TPU v7x, 32 devices: a whole 2x2x4 slice. The times are simulated.
32 devices in a mesh: gx: 4 (over z), gy: 4 (over x, core), gz: 2 (over y).
Axes of the slice: x: 2, y: 2, z: 4, core: 2. Of those that a mesh axis runs over, the one named last changes fastest.
Arguments:
- density: float32 [3, 64, 256, 256], P(None, 'gx', 'gy', 'gz'), may hold values from -6 to 6
- efficiency: float32 [64, 256, 256], P('gx', 'gy', 'gz'), may hold values from 0.5 to 2
Outputs:
- ionized: float32 [3, 64, 256, 256], P(None, 'gx', 'gy', 'gz')
All inputs are finite; a program needn't handle non-finite values.
Results may differ from a plain program's by a relative error of at most 0.00005.
Values sent between devices are 32-bit elements; how exact they have to be, the bound alone decides.
A program may use at most 128 MiB of HBM per device.

v0:
```python
import jax
import jax.numpy as jnp
from jax import lax
from jax.sharding import PartitionSpec as P

R_SMALL = 4
R_LARGE = 8


def extended(block, sides, width):
    for axis, dim in sides:
        count = lax.axis_size(axis)
        forward = [(i, i + 1) for i in range(count - 1)]
        forward.append((count - 1, 0))
        backward = [(target, source) for source, target in forward]
        low = lax.ppermute(
            lax.slice_in_dim(block, block.shape[dim] - width, None, axis=dim), axis, forward
        )
        high = lax.ppermute(lax.slice_in_dim(block, 0, width, axis=dim), axis, backward)
        block = jnp.concatenate([low, block, high], axis=dim)
    return block


def band_matrix(radius, length):
    rows = lax.broadcasted_iota(jnp.int32, (length, length + 2 * radius), 0)
    columns = lax.broadcasted_iota(jnp.int32, (length, length + 2 * radius), 1)
    offset = (columns - rows - radius).astype(jnp.float32)
    offsets = jnp.arange(-radius, radius + 1).astype(jnp.float32)
    raw_weights = 1.0 - (offsets / (radius + 1.0)) ** 2
    scale = jnp.sqrt(jnp.sum(raw_weights * raw_weights))
    inside = jnp.abs(offset) <= radius
    return jnp.where(inside, (1.0 - (offset / (radius + 1.0)) ** 2) / scale, 0.0)


def smooth_along(volume, radius, axis_dim):
    letters = "abcd"[: volume.ndim]
    length = volume.shape[axis_dim] - 2 * radius
    target = letters[:axis_dim] + "z" + letters[axis_dim + 1 :]
    formula = "z" + letters[axis_dim] + "," + letters + "->" + target
    return jnp.einsum(formula, band_matrix(radius, length), volume, precision=lax.Precision.HIGHEST)


def on_device(density, efficiency):
    trim = R_LARGE - R_SMALL
    slab = extended(density, (("gz", 3),), R_LARGE)
    small_part = smooth_along(slab[:, :, :, trim:-trim], R_SMALL, 3)
    large_part = smooth_along(slab, R_LARGE, 3)
    small_y = extended(small_part, (("gy", 2),), R_SMALL)
    large_y = extended(large_part, (("gy", 2),), R_LARGE)
    small_part = smooth_along(small_y, R_SMALL, 2)
    large_part = smooth_along(large_y, R_LARGE, 2)
    small_x = extended(small_part, (("gx", 1),), R_SMALL)
    large_x = extended(large_part, (("gx", 1),), R_LARGE)
    smooth_small = smooth_along(small_x, R_SMALL, 1)
    smooth_large = smooth_along(large_x, R_LARGE, 1)
    level_small = efficiency[None] * smooth_small - 0.3
    level_large = efficiency[None] * smooth_large - 0.1
    return jnp.clip(0.5 + 0.25 * jnp.maximum(level_small, level_large), 0.0, 1.0)


def solution(mesh):
    placed = (P(None, "gx", "gy", "gz"), P("gx", "gy", "gz"))
    return jax.shard_map(
        on_device, mesh=mesh, in_specs=placed, out_specs=P(None, "gx", "gy", "gz"), check_vma=False
    )
```

profile of v0, /device:TPU:0, one launch (start us, length us, event | category | flops | bytes accessed | tf_op | source)
XLA Modules:
  0.0 92.5 jit_solution(9772723643209291295)
XLA Ops:
  0.0 2.5 %fusion.171 = (f32[3,16,64,8]{3,2,1,0:T(8,128)S(1)}, f32[3,16,64,8]{3,2,1,0:T(8,128)S(1)}) fusion(f32[3,16,64,128]{3,2,1,0:T(8,128)} %param.2), kind=kLoop, calls=%fused_computation.178 | loop fusion | bytes 393216 | tf_op jit(solution)/shard_map/slice | solution.py:17
  2.9 3.0 %collective-permute-start.1 = (f32[3,16,64,8]{2,3,1,0:T(8,128)S(1)}, f32[3,16,64,8]{2,3,1,0:T(8,128)S(1)}, u32[]{:S(2)}, u32[]{:S(2)}) collective-permute-start(f32[3,16,64,8]{2,3,1,0:T(8,128)S(1)} %copy.22), channel_id=1, source_target_pairs={{1,0},{0,1},{3,2},{2,3},{5,4},{4,5},{7,6},{6,7},{9,8},{8,9},{11,10... | collective-permute-start | bytes 294920 | tf_op jit(solution)/shard_map/ppermute | solution.py:19
  5.9 1.1 %copy.21 = f32[3,16,64,8]{2,3,1,0:T(8,128)} copy(f32[3,16,64,8]{3,2,1,0:T(8,128)S(1)} %get-tuple-element.13) | data formatting | bytes 196608
  7.1 0.7 multiply_reduce_fusion.1
  8.4 0.7 multiply_reduce_fusion
  9.8 1.9 %collective-permute-done.1 = f32[3,16,64,8]{2,3,1,0:T(8,128)S(1)} collective-permute-done((f32[3,16,64,8]{2,3,1,0:T(8,128)S(1)}, f32[3,16,64,8]{2,3,1,0:T(8,128)S(1)}, u32[]{:S(2)}, u32[]{:S(2)}) %collective-permute-start.1) | collective-permute-done | bytes 98336 | tf_op jit(solution)/shard_map/ppermute | solution.py:19
  12.2 3.0 %collective-permute-done = f32[3,16,64,8]{2,3,1,0:T(8,128)} collective-permute-done((f32[3,16,64,8]{2,3,1,0:T(8,128)}, f32[3,16,64,8]{2,3,1,0:T(8,128)}, u32[]{:S(2)}, u32[]{:S(2)}) %collective-permute-start) | collective-permute-done | bytes 98336 | tf_op jit(solution)/shard_map/ppermute | solution.py:16
  15.2 2.6 %copy.10 = f32[3,16,64,8]{3,2,1,0:T(8,128)} copy(f32[3,16,64,8]{2,3,1,0:T(8,128)} %collective-permute-done) | data formatting | bytes 196608 | tf_op jit(solution)/shard_map/ppermute | solution.py:16
  17.7 2.7 %pad_maximum_fusion = f32[3,16,64,144]{3,2,1,0:T(8,128)S(1)} fusion(f32[3,16,64,8]{3,2,1,0:T(8,128)S(1)} %copy.11, f32[3,16,64,128]{3,2,1,0:T(8,128)S(1)} %copy-done, f32[3,16,64,8]{3,2,1,0:T(8,128)} %copy.10), kind=kLoop, calls=%fused_computation.2 | loop fusion | flops 884736 | bytes 3538944 | tf_op jit(solution)/shard_map/concatenate | solution.py:20
  20.4 2.7 %fusion = f32[3,16,64,128]{3,2,1,0:T(8,128)S(1)} fusion(f32[3,16,64,144]{3,2,1,0:T(8,128)S(1)} %pad_maximum_fusion, f32[]{:T(128)S(6)} %sqrt.4), kind=kOutput, calls=%fused_computation | convolution fusion | flops 641902592 | bytes 3342340 | tf_op jit(solution)/shard_map/zd,abcd->abcz/dot_general | solution.py:40
  23.7 2.7 %fusion.32 = f32[3,16,64,128]{3,2,1,0:T(8,128)S(1)} fusion(f32[3,16,64,144]{3,2,1,0:T(8,128)S(1)} %pad_maximum_fusion, f32[]{:T(128)S(6)} %sqrt.5), kind=kOutput, calls=%fused_computation.31 | convolution fusion | flops 679661568 | bytes 3342340 | tf_op jit(solution)/shard_map/zd,abcd->abcz/dot_general | solution.py:40
  26.4 1.6 %collective-permute-start.7 = (f32[3,16,8,128]{3,2,1,0:T(8,128)S(1)}, f32[3,16,8,128]{3,2,1,0:T(8,128)S(1)}, u32[]{:S(2)}, u32[]{:S(2)}) collective-permute-start(f32[3,16,8,128]{3,2,1,0:T(8,128)S(1)} %get-tuple-element.8), channel_id=1, source_target_pairs={{2,0},{4,2},{6,4},{0,6},{3,1},{5,3},{7,5},{1,7},{10,8},{12,10},{14... | collective-permute-start | bytes 589832 | tf_op jit(solution)/shard_map/ppermute | solution.py:19
  28.5 1.8 %fusion.26 = f32[3,16,64,128]{3,2,1,0:T(8,128)S(1)} fusion(f32[3,16,4,128]{3,2,1,0:T(4,128)S(1)} %collective-permute-done.3, f32[3,16,64,128]{3,2,1,0:T(8,128)S(1)} %fusion, f32[3,16,4,128]{3,2,1,0:T(4,128)S(1)} %collective-permute-done.2, f32[]{:T(128)S(6)} %sqrt.4), kind=kOutput, calls=%fused_computation.29 | convolution fusion | flops 340669440 | bytes 3342340 | tf_op jit(solution)/shard_map/zc,abcd->abzd/dot_general | solution.py:40
  30.4 3.7 %collective-permute-start.5 = (f32[3,4,64,128]{3,2,1,0:T(8,128)S(1)}, f32[3,4,64,128]{3,2,1,0:T(8,128)S(1)}, u32[]{:S(2)}, u32[]{:S(2)}) collective-permute-start(f32[3,4,64,128]{3,2,1,0:T(8,128)S(1)} %get-tuple-element.10), channel_id=1, source_target_pairs={{8,0},{16,8},{24,16},{0,24},{9,1},{17,9},{25,17},{1,25},{10,2},{18... | collective-permute-start | bytes 1179656 | tf_op jit(solution)/shard_map/ppermute | solution.py:19
  34.1 1.1 %collective-permute-done.6 = f32[3,16,8,128]{3,2,1,0:T(8,128)S(1)} collective-permute-done((f32[3,16,8,128]{3,2,1,0:T(8,128)S(1)}, f32[3,16,8,128]{3,2,1,0:T(8,128)S(1)}, u32[]{:S(2)}, u32[]{:S(2)}) %collective-permute-start.6) | collective-permute-done | bytes 196640 | tf_op jit(solution)/shard_map/ppermute | solution.py:16
  35.2 1.7 %fusion.29 = f32[3,16,64,128]{3,2,1,0:T(8,128)S(1)} fusion(f32[3,16,8,128]{3,2,1,0:T(8,128)S(1)} %collective-permute-done.7, f32[3,16,64,128]{3,2,1,0:T(8,128)S(1)} %fusion.32, f32[3,16,8,128]{3,2,1,0:T(8,128)S(1)} %collective-permute-done.6, f32[]{:T(128)S(6)} %sqrt.5), kind=kOutput, calls=%fused_computation.30 | convolution fusion | flops 378521600 | bytes 3538948 | tf_op jit(solution)/shard_map/zc,abcd->abzd/dot_general | solution.py:40
  37.0 3.7 %collective-permute-start.9 = (f32[3,8,64,128]{3,2,1,0:T(8,128)S(1)}, f32[3,8,64,128]{3,2,1,0:T(8,128)S(1)}, u32[]{:S(2)}, u32[]{:S(2)}) collective-permute-start(f32[3,8,64,128]{3,2,1,0:T(8,128)S(1)} %get-tuple-element.6), channel_id=1, source_target_pairs={{8,0},{16,8},{24,16},{0,24},{9,1},{17,9},{25,17},{1,25},{10,2},{18... | collective-permute-start | bytes 2359304 | tf_op jit(solution)/shard_map/ppermute | solution.py:19
  41.0 2.5 %collective-permute-done.5 = f32[3,4,64,128]{3,2,1,0:T(8,128)S(1)} collective-permute-done((f32[3,4,64,128]{3,2,1,0:T(8,128)S(1)}, f32[3,4,64,128]{3,2,1,0:T(8,128)S(1)}, u32[]{:S(2)}, u32[]{:S(2)}) %collective-permute-start.5) | collective-permute-done | bytes 393248 | tf_op jit(solution)/shard_map/ppermute | solution.py:19
  43.5 9.4 %collective-permute-done.4 = f32[3,4,64,128]{3,2,1,0:T(8,128)S(1)} collective-permute-done((f32[3,4,64,128]{3,2,1,0:T(8,128)S(1)}, f32[3,4,64,128]{3,2,1,0:T(8,128)S(1)}, u32[]{:S(2)}, u32[]{:S(2)}) %collective-permute-start.4) | collective-permute-done | bytes 393248 | tf_op jit(solution)/shard_map/ppermute | solution.py:16
  53.2 2.9 %fusion.4 = f32[3,64,128,16]{2,3,1,0:T(8,128)S(1)} fusion(f32[3,24,64,128]{3,2,1,0:T(8,128)S(1)} %pad_maximum_fusion.2, f32[]{:T(128)S(6)} %sqrt.4), kind=kOutput, calls=%fused_computation.7 | convolution fusion | flops 113250048 | bytes 3932164 | tf_op jit(solution)/shard_map/zb,abcd->azcd/dot_general | solution.py:40
  56.1 12.7 %collective-permute-done.9 = f32[3,8,64,128]{3,2,1,0:T(8,128)S(1)} collective-permute-done((f32[3,8,64,128]{3,2,1,0:T(8,128)S(1)}, f32[3,8,64,128]{3,2,1,0:T(8,128)S(1)}, u32[]{:S(2)}, u32[]{:S(2)}) %collective-permute-start.9) | collective-permute-done | bytes 786464 | tf_op jit(solution)/shard_map/ppermute | solution.py:19
  68.8 17.7 %collective-permute-done.8 = f32[3,8,64,128]{3,2,1,0:T(8,128)S(1)} collective-permute-done((f32[3,8,64,128]{3,2,1,0:T(8,128)S(1)}, f32[3,8,64,128]{3,2,1,0:T(8,128)S(1)}, u32[]{:S(2)}, u32[]{:S(2)}) %collective-permute-start.8) | collective-permute-done | bytes 786464 | tf_op jit(solution)/shard_map/ppermute | solution.py:16
  87.0 3.9 %fusion.22 = f32[3,16,64,128]{3,1,2,0:T(8,128)S(1)} fusion(f32[3,64,128,16]{2,3,1,0:T(8,128)S(1)} %fusion.4, f32[3,32,64,128]{3,2,1,0:T(8,128)S(1)} %pad_maximum_fusion.1, f32[16,64,128]{2,0,1:T(8,128)S(1)} %copy.7, f32[]{:T(128)S(6)} %sqrt.5), kind=kOutput, calls=%fused_computation.26 | convolution fusion | flops 154145792 | bytes 6815748 | tf_op jit(solution)/shard_map/zb,abcd->azcd/dot_general | solution.py:40
  90.9 1.6 %copy.14 = f32[3,16,64,128]{3,2,1,0:T(8,128)} copy(f32[3,16,64,128]{3,1,2,0:T(8,128)S(1)} %fusion.22) | data formatting | bytes 3145728 | tf_op jit(solution)/shard_map/jit(clip)/min | solution.py:58
  (22 shorter events, 3.3 us)
Async XLA Ops:
  2.9 8.8 %collective-permute-start.1 = (f32[3,16,64,8]{2,3,1,0:T(8,128)S(1)}, f32[3,16,64,8]{2,3,1,0:T(8,128)S(1)}, u32[]{:S(2)}, u32[]{:S(2)}) collective-permute-start(f32[3,16,64,8]{2,3,1,0:T(8,128)S(1)} %copy.22), channel_id=1, source_target_pairs={{1,0},{0,1},{3,2},{2,3},{5,4},{4,5},{7,6},{6,7},{9,8},{8,9},{11,10... | collective-permute-start | bytes 294920 | tf_op jit(solution)/shard_map/ppermute | solution.py:19
  7.1 8.1 %collective-permute-start = (f32[3,16,64,8]{2,3,1,0:T(8,128)}, f32[3,16,64,8]{2,3,1,0:T(8,128)}, u32[]{:S(2)}, u32[]{:S(2)}) collective-permute-start(f32[3,16,64,8]{2,3,1,0:T(8,128)} %copy.21), channel_id=1, source_target_pairs={{0,1},{1,0},{2,3},{3,2},{4,5},{5,4},{6,7},{7,6},{8,9},{9,8},{10,11... | collective-permute-start | bytes 294920 | tf_op jit(solution)/shard_map/ppermute | solution.py:16
  9.8 7.9 %copy-start = (f32[3,16,64,128]{3,2,1,0:T(8,128)S(1)}, f32[3,16,64,128]{3,2,1,0:T(8,128)}, u32[]{:S(2)}) copy-start(f32[3,16,64,128]{3,2,1,0:T(8,128)} %param.2) | copy-start | bytes 4718596
  23.1 4.9 %collective-permute-start.3 = (f32[3,16,4,128]{3,2,1,0:T(4,128)S(1)}, f32[3,16,4,128]{3,2,1,0:T(4,128)S(1)}, u32[]{:S(2)}, u32[]{:S(2)}) collective-permute-start(f32[3,16,4,128]{3,2,1,0:T(4,128)S(1)} %get-tuple-element.12), channel_id=1, source_target_pairs={{2,0},{4,2},{6,4},{0,6},{3,1},{5,3},{7,5},{1,7},{10,8},{12,10},{14... | collective-permute-start | bytes 294920 | tf_op jit(solution)/shard_map/ppermute | solution.py:19
  23.5 5.1 %collective-permute-start.2 = (f32[3,16,4,128]{3,2,1,0:T(4,128)S(1)}, f32[3,16,4,128]{3,2,1,0:T(4,128)S(1)}, u32[]{:S(2)}, u32[]{:S(2)}) collective-permute-start(f32[3,16,4,128]{3,2,1,0:T(4,128)S(1)} %get-tuple-element.11), channel_id=1, source_target_pairs={{0,2},{2,4},{4,6},{6,0},{1,3},{3,5},{5,7},{7,1},{8,10},{10,12},{12... | collective-permute-start | bytes 294920 | tf_op jit(solution)/shard_map/ppermute | solution.py:16
  26.4 7.6 %collective-permute-start.7 = (f32[3,16,8,128]{3,2,1,0:T(8,128)S(1)}, f32[3,16,8,128]{3,2,1,0:T(8,128)S(1)}, u32[]{:S(2)}, u32[]{:S(2)}) collective-permute-start(f32[3,16,8,128]{3,2,1,0:T(8,128)S(1)} %get-tuple-element.8), channel_id=1, source_target_pairs={{2,0},{4,2},{6,4},{0,6},{3,1},{5,3},{7,5},{1,7},{10,8},{12,10},{14... | collective-permute-start | bytes 589832 | tf_op jit(solution)/shard_map/ppermute | solution.py:19
  28.0 7.2 %collective-permute-start.6 = (f32[3,16,8,128]{3,2,1,0:T(8,128)S(1)}, f32[3,16,8,128]{3,2,1,0:T(8,128)S(1)}, u32[]{:S(2)}, u32[]{:S(2)}) collective-permute-start(f32[3,16,8,128]{3,2,1,0:T(8,128)S(1)} %get-tuple-element.7), channel_id=1, source_target_pairs={{0,2},{2,4},{4,6},{6,0},{1,3},{3,5},{5,7},{7,1},{8,10},{10,12},{12... | collective-permute-start | bytes 589832 | tf_op jit(solution)/shard_map/ppermute | solution.py:16
  30.4 13.1 %collective-permute-start.5 = (f32[3,4,64,128]{3,2,1,0:T(8,128)S(1)}, f32[3,4,64,128]{3,2,1,0:T(8,128)S(1)}, u32[]{:S(2)}, u32[]{:S(2)}) collective-permute-start(f32[3,4,64,128]{3,2,1,0:T(8,128)S(1)} %get-tuple-element.10), channel_id=1, source_target_pairs={{8,0},{16,8},{24,16},{0,24},{9,1},{17,9},{25,17},{1,25},{10,2},{18... | collective-permute-start | bytes 1179656 | tf_op jit(solution)/shard_map/ppermute | solution.py:19
  34.1 18.8 %collective-permute-start.4 = (f32[3,4,64,128]{3,2,1,0:T(8,128)S(1)}, f32[3,4,64,128]{3,2,1,0:T(8,128)S(1)}, u32[]{:S(2)}, u32[]{:S(2)}) collective-permute-start(f32[3,4,64,128]{3,2,1,0:T(8,128)S(1)} %get-tuple-element.9), channel_id=1, source_target_pairs={{0,8},{8,16},{16,24},{24,0},{1,9},{9,17},{17,25},{25,1},{2,10},{10... | collective-permute-start | bytes 1179656 | tf_op jit(solution)/shard_map/ppermute | solution.py:16
  36.9 3.8 %copy-start.1 = (f32[16,64,128]{2,1,0:T(8,128)S(1)}, f32[16,64,128]{2,1,0:T(8,128)}, u32[]{:S(2)}) copy-start(f32[16,64,128]{2,1,0:T(8,128)} %param.3) | copy-start | bytes 1572868
  37.0 31.8 %collective-permute-start.9 = (f32[3,8,64,128]{3,2,1,0:T(8,128)S(1)}, f32[3,8,64,128]{3,2,1,0:T(8,128)S(1)}, u32[]{:S(2)}, u32[]{:S(2)}) collective-permute-start(f32[3,8,64,128]{3,2,1,0:T(8,128)S(1)} %get-tuple-element.6), channel_id=1, source_target_pairs={{8,0},{16,8},{24,16},{0,24},{9,1},{17,9},{25,17},{1,25},{10,2},{18... | collective-permute-start | bytes 2359304 | tf_op jit(solution)/shard_map/ppermute | solution.py:19
  40.7 45.9 %collective-permute-start.8 = (f32[3,8,64,128]{3,2,1,0:T(8,128)S(1)}, f32[3,8,64,128]{3,2,1,0:T(8,128)S(1)}, u32[]{:S(2)}, u32[]{:S(2)}) collective-permute-start(f32[3,8,64,128]{3,2,1,0:T(8,128)S(1)} %get-tuple-element.5), channel_id=1, source_target_pairs={{0,8},{8,16},{16,24},{24,0},{1,9},{9,17},{17,25},{25,1},{2,10},{10... | collective-permute-start | bytes 2359304 | tf_op jit(solution)/shard_map/ppermute | solution.py:16
where the time goes:
time: 92.7 us; the launch traced here: 92.5 us
  waiting for transfers between devices  48.9 us (53%)
  matrix products  15.7 us (17%)
  starting transfers between devices  12.5 us (13%)
  local copies, waits for them, and re-layouts  9.29 us (10%)
  other arithmetic  4.69 us (5%)
  between operations  1.49 us (2%)
    ppermute x5, waiting for transfers between devices, extended(): lax.ppermute(lax.slice_in_dim(block, block.shape[dim] - width, None, axis...  31.7 us
    ppermute x5, waiting for transfers between devices, extended(): lax.ppermute(lax.slice_in_dim(block, 0, width, axis=dim), axis, backward)  17.1 us
    dot_general x6, matrix products, smooth_along(): jnp.einsum(formula, band_matrix(radius, length), volume, precision=lax.Pr...  15.7 us
    ppermute x5, starting transfers between devices, extended(): lax.ppermute(lax.slice_in_dim(block, 0, width, axis=dim), axis, backward)  12.3 us
    concatenate x3, other arithmetic, extended(): block = jnp.concatenate([low, block, high], axis=dim)  3.35 us
    slice x5, local copies, waits for them, and re-layouts, extended(): lax.slice_in_dim(block, block.shape[dim] - width, None, axis=dim)  2.73 us
    ppermute x1, local copies, waits for them, and re-layouts, extended(): lax.ppermute(lax.slice_in_dim(block, block.shape[dim] - width, None, axis...  2.56 us
    unnamed x7, local copies, waits for them, and re-layouts  1.9 us
  transfers between devices with their start and end apart: 10, of which 8 were waited for; matrix products, arithmetic and copies ran while one was open for 14% of the time, Pallas kernels for 0%

commit v1 on v0

v1 whole, which is shorter than its diff:
```python
import functools
import math

import jax
import jax.numpy as jnp
from jax import lax
from jax.experimental import pallas as pl
from jax.experimental.pallas import tpu as pltpu
from jax.sharding import PartitionSpec as P

R_SMALL = 4
R_LARGE = 8
RADII = (R_SMALL, R_LARGE)
H = R_LARGE
GROUP = 16
F32 = jnp.float32
BF16 = jnp.bfloat16
MESH = pl.DeviceIdType.MESH


def scale_of(radius):
    raw = [(radius + 1) ** 2 - k * k for k in range(-radius, radius + 1)]
    return 1.0 / math.sqrt(sum(value * value for value in raw)) ** 3


def band(offset, radius):
    value = (radius + 1) ** 2 - offset * offset
    return jnp.where(jnp.abs(offset) <= radius, value, 0).astype(F32).astype(BF16)


def split(value):
    high = value.astype(BF16)
    return high, (value - high.astype(F32)).astype(BF16)


def iota(shape, dim):
    return lax.broadcasted_iota(jnp.int32, shape, dim)


def kernel(dens, eff, out, ext, effv, xb, zb, zm, zsend, zrecv, wy, wm, wh, outv,
           x_send, x_recv, y_send, y_recv, f_send, f_recv, z_send, z_recv,
           own_sem, eff_sem, out_sem):
    snaps, nx, ny, nz = dens.shape
    rows = ny + 2 * H
    groups = rows // GROUP
    near = {}
    for axis in ("gx", "gy", "gz"):
        count = lax.axis_size(axis)
        me = lax.axis_index(axis)
        near[axis] = (lax.rem(me + 1, count), lax.rem(me + count - 1, count))

    def own_copy(s):
        return pltpu.make_async_copy(
            dens.at[s], ext.at[s, pl.ds(H, nx), pl.ds(H, ny)], own_sem.at[s])

    eff_copy = pltpu.make_async_copy(eff, effv, eff_sem)

    def out_copy(s):
        return pltpu.make_async_copy(outv.at[s], out.at[s], out_sem.at[s])

    def group_rows(g):
        if g == 0:
            return 0, H
        if g == groups - 1:
            return ny - H, H
        return g * GROUP - H, GROUP

    def x_copy(s, g, d):
        start, size = group_rows(g)
        source = nx - H if d == 0 else 0
        target = 0 if d == 0 else nx + H
        return pltpu.make_async_remote_copy(
            src_ref=dens.at[s, pl.ds(source, H), pl.ds(start, size)],
            dst_ref=ext.at[s, pl.ds(target, H), pl.ds(H + start, size)],
            send_sem=x_send.at[s, g, d], recv_sem=x_recv.at[s, g, d],
            device_id={"gx": near["gx"][d]}, device_id_type=MESH)

    def y_copy(s, d):
        source = ny - H if d == 0 else 0
        target = 0 if d == 0 else ny + H
        return pltpu.make_async_remote_copy(
            src_ref=dens.at[s, :, pl.ds(source, H)],
            dst_ref=ext.at[s, pl.ds(H, nx), pl.ds(target, H)],
            send_sem=y_send.at[s, d], recv_sem=y_recv.at[s, d],
            device_id={"gy": near["gy"][d]}, device_id_type=MESH)

    def f_copy(s, q, d):
        planes = 0 if q == 0 else nx + H
        source = ny if d == 0 else H
        target = 0 if d == 0 else ny + H
        return pltpu.make_async_remote_copy(
            src_ref=ext.at[s, pl.ds(planes, H), pl.ds(source, H)],
            dst_ref=ext.at[s, pl.ds(planes, H), pl.ds(target, H)],
            send_sem=f_send.at[s, q, d], recv_sem=f_recv.at[s, q, d],
            device_id={"gy": near["gy"][d]}, device_id_type=MESH)

    def z_copy(s, d):
        return pltpu.make_async_remote_copy(
            src_ref=zsend.at[s, d], dst_ref=zrecv.at[s, d],
            send_sem=z_send.at[s, d], recv_sem=z_recv.at[s, d],
            device_id={"gz": near["gz"][d]}, device_id_type=MESH)

    for s in range(snaps):
        own_copy(s).start()
    eff_copy.start()

    barrier = pltpu.get_barrier_semaphore()
    for axis in ("gx", "gy", "gz"):
        for d in range(2):
            pl.semaphore_signal(
                barrier, inc=1, device_id={axis: near[axis][d]}, device_id_type=MESH)
    pl.semaphore_wait(barrier, 6)

    edge = (0, groups - 1)
    inner = tuple(range(1, groups - 1))
    for s in range(snaps):
        for g in edge:
            for d in range(2):
                x_copy(s, g, d).start()
    for s in range(snaps):
        for d in range(2):
            y_copy(s, d).start()
    for s in range(snaps):
        for g in inner:
            for d in range(2):
                x_copy(s, g, d).start()

    for f, radius in enumerate(RADII):
        shape = (ny, rows)
        along = band(iota(shape, 1) - iota(shape, 0) - H, radius)
        wy[f] = jnp.concatenate([along, along], axis=1)
        shape = (nz, nz)
        along = band(iota(shape, 1) - iota(shape, 0), radius)
        wm[f] = jnp.concatenate([along, along], axis=0)
        shape = (nx * H, nz)
        slot = lax.div(iota(shape, 0), H)
        cell = lax.rem(iota(shape, 0), H)
        lane = iota(shape, 1)
        low = band(cell - H - lane, radius)
        high = band(cell + nz - lane, radius)
        zero = jnp.zeros_like(low)
        for p in range(nx):
            low_p = jnp.where(slot == p, low, zero)
            high_p = jnp.where(slot == (p + 1) % nx, high, zero)
            wh[f, p // 2, pl.ds(0, nx * H), pl.ds((p % 2) * nz, nz)] = low_p
            wh[f, p // 2, pl.ds(nx * H, nx * H), pl.ds((p % 2) * nz, nz)] = high_p

    for s in range(snaps):
        for d, g in ((0, groups - 1), (1, 0)):
            for q in range(2):
                x_copy(s, g, q).wait_recv()
                f_copy(s, q, d).start()

    def smooth_x(s, g):
        base = g * GROUP

        def one(i, carry):
            def plane(k):
                return ext[s, i + (H + k), pl.ds(base, GROUP)]

            center = plane(0)
            sums = [center * float((radius + 1) ** 2) for radius in RADII]
            for k in range(1, R_LARGE + 1):
                pair = plane(-k) + plane(k)
                for f, radius in enumerate(RADII):
                    if k <= radius:
                        sums[f] = sums[f] + pair * float((radius + 1) ** 2 - k * k)
            for f in range(2):
                high, low = split(sums[f])
                xb[f, i, pl.ds(base, GROUP)] = high
                xb[f, i, pl.ds(rows + base, GROUP)] = low
            return carry

        lax.fori_loop(0, nx, one, 0, unroll=4)

    slots = lax.div(iota((ny, nz), 1), H)

    def smooth_y(s):
        for f in range(2):
            up = jnp.zeros((ny, nz), F32)
            down = jnp.zeros((ny, nz), F32)
            for p in range(0, nx, 2):
                both = jnp.concatenate([xb[f, p], xb[f, p + 1]], axis=1)
                done = jnp.dot(wy[f], both, preferred_element_type=F32)
                for j in range(2):
                    value = done[:, j * nz:(j + 1) * nz]
                    rolled = pltpu.roll(value, ((p + j + 1) * H) % nz, 1)
                    up = jnp.where(slots == p + j, rolled, up)
                    down = jnp.where(slots == (p + j + 1) % nx, rolled, down)
                    high, low = split(value)
                    zb[f, p + j, :, pl.ds(0, nz)] = high
                    zb[f, p + j, :, pl.ds(nz, nz)] = low
            zsend[s, 0, pl.ds(f * ny, ny)] = up
            zsend[s, 1, pl.ds(f * ny, ny)] = down
        for d in range(2):
            z_copy(s, d).start()

    def main_z(s):
        slot = s % 2
        for f in range(2):
            for p in range(0, nx, 4):
                block = zb[f, pl.ds(p, 4)].reshape(4 * ny, 2 * nz)
                done = jnp.dot(block, wm[f], preferred_element_type=F32)
                zm[slot, f, pl.ds(p, 4)] = done.reshape(4, ny, nz)

    def finish(s):
        slot = s % 2
        for d in range(2):
            z_copy(s, d).wait_recv()
        halves = []
        for f in range(2):
            packed = jnp.concatenate(
                [zrecv[s, 0, pl.ds(f * ny, ny)], zrecv[s, 1, pl.ds(f * ny, ny)]], axis=1)
            halves.append(jnp.concatenate(split(packed), axis=0))
        for p in range(0, nx, 2):
            level = [None, None]
            for f, (radius, less) in enumerate(zip(RADII, (0.3, 0.1))):
                done = jnp.dot(halves[f], wh[f, p // 2], preferred_element_type=F32)
                done = done[:ny] + done[ny:]
                pair = []
                for j in range(2):
                    smooth = (zm[slot, f, p + j] + done[:, j * nz:(j + 1) * nz]) * scale_of(radius)
                    pair.append(effv[p + j] * smooth - less)
                level[f] = pair
            for j in range(2):
                outv[s, p + j] = jnp.maximum(level[0][j], level[1][j])
        out_copy(s).start()

    for s in range(snaps):
        own_copy(s).wait()
        for d in range(2):
            y_copy(s, d).wait_recv()
            for q in range(2):
                f_copy(s, q, d).wait_recv()
        for g in edge:
            smooth_x(s, g)
        for g in inner:
            for d in range(2):
                x_copy(s, g, d).wait_recv()
            smooth_x(s, g)
        smooth_y(s)
        main_z(s)
        if s == 0:
            eff_copy.wait()
        else:
            finish(s - 1)
    finish(snaps - 1)

    for s in range(snaps):
        for d in range(2):
            for g in range(groups):
                x_copy(s, g, d).wait_send()
            y_copy(s, d).wait_send()
            z_copy(s, d).wait_send()
            for q in range(2):
                f_copy(s, q, d).wait_send()
        out_copy(s).wait()


def on_device(density, efficiency):
    snaps, nx, ny, nz = density.shape
    rows = ny + 2 * H
    groups = rows // GROUP
    dma = pltpu.SemaphoreType.DMA
    level = pl.pallas_call(
        kernel,
        out_shape=jax.ShapeDtypeStruct(density.shape, F32),
        in_specs=[pl.BlockSpec(memory_space=pl.ANY)] * 2,
        out_specs=pl.BlockSpec(memory_space=pl.ANY),
        scratch_shapes=[
            pltpu.VMEM((snaps, nx + 2 * H, rows, nz), F32),
            pltpu.VMEM((nx, ny, nz), F32),
            pltpu.VMEM((2, nx, 2 * rows, nz), BF16),
            pltpu.VMEM((2, nx, ny, 2 * nz), BF16),
            pltpu.VMEM((2, 2, nx, ny, nz), F32),
            pltpu.VMEM((snaps, 2, 2 * ny, nx * H), F32),
            pltpu.VMEM((snaps, 2, 2 * ny, nx * H), F32),
            pltpu.VMEM((2, ny, 2 * rows), BF16),
            pltpu.VMEM((2, 2 * nz, nz), BF16),
            pltpu.VMEM((2, nx // 2, 2 * nx * H, 2 * nz), BF16),
            pltpu.VMEM((snaps, nx, ny, nz), F32),
            dma((snaps, groups, 2)), dma((snaps, groups, 2)),
            dma((snaps, 2)), dma((snaps, 2)),
            dma((snaps, 2, 2)), dma((snaps, 2, 2)),
            dma((snaps, 2)), dma((snaps, 2)),
            dma((snaps,)), dma, dma((snaps,)),
        ],
        compiler_params=pltpu.CompilerParams(
            collective_id=0, has_side_effects=True),
    )(density, efficiency)
    return jnp.clip(0.5 + 0.25 * level, 0.0, 1.0)


def solution(mesh):
    placed = (P(None, "gx", "gy", "gz"), P("gx", "gy", "gz"))
    return jax.shard_map(
        on_device, mesh=mesh, in_specs=placed, out_specs=P(None, "gx", "gy", "gz"), check_vma=False
    )
```

time: 92.7 us -> 51.7 us (0.56)
  waiting for transfers between devices: 48.9 us -> 0 us
  Pallas kernels: 0 us -> 48.7 us
  matrix products: 15.7 us -> 0 us
  starting transfers between devices: 12.5 us -> 0 us
  local copies, waits for them, and re-layouts: 9.29 us -> 0 us
  other arithmetic: 4.69 us -> 2.86 us
  between operations: 1.49 us -> 0.01 us
    ppermute x10 -> x0, waiting for transfers between devices: 48.9 us -> none  [the longest x5 31.7 us: extended(): lax.ppermute(lax.slice_in_dim(block, block.shape[dim] - width, None, axis...]
    pallas_call x0 -> x1, Pallas kernels: none -> 48.7 us  [on_device(): pl.pallas_call(kernel, out_shape=jax.ShapeDtypeStruct(density.shape, F32)...]
    dot_general x6 -> x0, matrix products: 15.7 us -> none  [smooth_along(): jnp.einsum(formula, band_matrix(radius, length), volume, precision=lax.Pr...]
    ppermute x10 -> x0, starting transfers between devices: 12.5 us -> none  [the longest x5 12.3 us: extended(): lax.ppermute(lax.slice_in_dim(block, 0, width, axis=dim), axis, backward)]
    concatenate x3 -> x0, other arithmetic: 3.35 us -> none  [extended(): block = jnp.concatenate([low, block, high], axis=dim)]
    ppermute x2 -> x0, local copies, waits for them, and re-layouts: 3.04 us -> none  [the longest x1 2.56 us: extended(): lax.ppermute(lax.slice_in_dim(block, block.shape[dim] - width, None, axis...]
    min x0 -> x1, other arithmetic: none -> 2.86 us  [on_device(): return jnp.clip(0.5 + 0.25 * level, 0.0, 1.0)]
    slice x5 -> x0, local copies, waits for them, and re-layouts: 2.73 us -> none  [extended(): lax.slice_in_dim(block, block.shape[dim] - width, None, axis=dim)]
  transfers between devices with their start and end apart: 10 -> 0, of which waited for: 8 -> 0; matrix products, arithmetic and copies ran while one was open for 14% -> 0% of each run, Pallas kernels for 0% -> 0%
where the time goes in v1:
time: 51.7 us; the launch traced here: 51.6 us
  Pallas kernels  48.7 us (94%)
  other arithmetic  2.86 us (6%)
    pallas_call x1, Pallas kernels, on_device(): pl.pallas_call(kernel, out_shape=jax.ShapeDtypeStruct(density.shape, F32)...  48.7 us
    min x1, other arithmetic, on_device(): return jnp.clip(0.5 + 0.25 * level, 0.0, 1.0)  2.86 us

profile of v1, /device:TPU:0, one launch (start us, length us, event | category | flops | bytes accessed | tf_op | source)
XLA Modules:
  0.0 51.6 jit_solution(2605057801741552583)
XLA Ops:
  0.0 48.7 %shard_map.28 = f32[3,16,64,128]{3,2,1,0:T(8,128)} custom-call(f32[3,16,64,128]{3,2,1,0:T(8,128)} %dens.1, f32[16,64,128]{2,1,0:T(8,128)} %eff.1), custom_call_target="tpu_custom_call" | custom-call | tf_op jit(solution)/shard_map/pallas_call | solution.py:265
  48.7 2.9 %add_clamp_fusion = f32[3,16,64,128]{3,2,1,0:T(8,128)} fusion(f32[3,16,64,128]{3,2,1,0:T(8,128)} %shard_map.28), kind=kLoop, calls=%fused_computation | loop fusion | flops 1179648 | bytes 3145728 | tf_op jit(solution)/shard_map/jit(clip)/min | solution.py:291

commit v2 on v1

--- a/solution.py
+++ b/solution.py
@@ -13,6 +13,7 @@
 RADII = (R_SMALL, R_LARGE)
 H = R_LARGE
 GROUP = 16
+STRIP = 32
 F32 = jnp.float32
 BF16 = jnp.bfloat16
 MESH = pl.DeviceIdType.MESH
@@ -37,12 +38,15 @@
     return lax.broadcasted_iota(jnp.int32, shape, dim)
 
 
-def kernel(dens, eff, out, ext, effv, xb, zb, zm, zsend, zrecv, wy, wm, wh, outv,
+def kernel(dens, eff, outv, ext, effv, xb, zb, zm, zsend, zrecv, wy, wm, wh,
            x_send, x_recv, y_send, y_recv, f_send, f_recv, z_send, z_recv,
            own_sem, eff_sem, out_sem):
+    out = None
     snaps, nx, ny, nz = dens.shape
     rows = ny + 2 * H
     groups = rows // GROUP
+    strips = ny // STRIP
+    wide = STRIP + 2 * H
     near = {}
     for axis in ("gx", "gy", "gz"):
         count = lax.axis_size(axis)
@@ -55,8 +59,10 @@
 
     eff_copy = pltpu.make_async_copy(eff, effv, eff_sem)
 
-    def out_copy(s):
-        return pltpu.make_async_copy(outv.at[s], out.at[s], out_sem.at[s])
+    def out_copy(u):
+        s, h = divmod(u, strips)
+        part = pl.ds(h * STRIP, STRIP)
+        return pltpu.make_async_copy(outv.at[s, :, part], out.at[s, :, part], out_sem.at[u])
 
     def group_rows(g):
         if g == 0:
@@ -94,10 +100,10 @@
             send_sem=f_send.at[s, q, d], recv_sem=f_recv.at[s, q, d],
             device_id={"gy": near["gy"][d]}, device_id_type=MESH)
 
-    def z_copy(s, d):
+    def z_copy(u, d):
         return pltpu.make_async_remote_copy(
-            src_ref=zsend.at[s, d], dst_ref=zrecv.at[s, d],
-            send_sem=z_send.at[s, d], recv_sem=z_recv.at[s, d],
+            src_ref=zsend.at[u, d], dst_ref=zrecv.at[u, d],
+            send_sem=z_send.at[u, d], recv_sem=z_recv.at[u, d],
             device_id={"gz": near["gz"][d]}, device_id_type=MESH)
 
     for s in range(snaps):
@@ -126,7 +132,7 @@
                 x_copy(s, g, d).start()
 
     for f, radius in enumerate(RADII):
-        shape = (ny, rows)
+        shape = (STRIP, wide)
         along = band(iota(shape, 1) - iota(shape, 0) - H, radius)
         wy[f] = jnp.concatenate([along, along], axis=1)
         shape = (nz, nz)
@@ -173,14 +179,18 @@
 
         lax.fori_loop(0, nx, one, 0, unroll=4)
 
-    slots = lax.div(iota((ny, nz), 1), H)
-
-    def smooth_y(s):
+    slots = lax.div(iota((STRIP, nz), 1), H)
+
+    def smooth_y(u):
+        base = (u % strips) * STRIP
         for f in range(2):
-            up = jnp.zeros((ny, nz), F32)
-            down = jnp.zeros((ny, nz), F32)
+            up = jnp.zeros((STRIP, nz), F32)
+            down = jnp.zeros((STRIP, nz), F32)
             for p in range(0, nx, 2):
-                both = jnp.concatenate([xb[f, p], xb[f, p + 1]], axis=1)
+                both = jnp.concatenate(
+                    [jnp.concatenate([xb[f, p + j, pl.ds(base, wide)],
+                                      xb[f, p + j, pl.ds(rows + base, wide)]], axis=0)
+                     for j in range(2)], axis=1)
                 done = jnp.dot(wy[f], both, preferred_element_type=F32)
                 for j in range(2):
                     value = done[:, j * nz:(j + 1) * nz]
@@ -190,42 +200,47 @@
                     high, low = split(value)
                     zb[f, p + j, :, pl.ds(0, nz)] = high
                     zb[f, p + j, :, pl.ds(nz, nz)] = low
-            zsend[s, 0, pl.ds(f * ny, ny)] = up
-            zsend[s, 1, pl.ds(f * ny, ny)] = down
-        for d in range(2):
-            z_copy(s, d).start()
-
-    def main_z(s):
-        slot = s % 2
+            zsend[u, 0, pl.ds(f * STRIP, STRIP)] = up
+            zsend[u, 1, pl.ds(f * STRIP, STRIP)] = down
+        for d in range(2):
+            z_copy(u, d).start()
+
+    def main_z(u):
+        slot = u % 2
         for f in range(2):
-            for p in range(0, nx, 4):
-                block = zb[f, pl.ds(p, 4)].reshape(4 * ny, 2 * nz)
+            for p in range(0, nx, 8):
+                block = zb[f, pl.ds(p, 8)].reshape(8 * STRIP, 2 * nz)
                 done = jnp.dot(block, wm[f], preferred_element_type=F32)
-                zm[slot, f, pl.ds(p, 4)] = done.reshape(4, ny, nz)
-
-    def finish(s):
-        slot = s % 2
-        for d in range(2):
-            z_copy(s, d).wait_recv()
+                zm[slot, f, pl.ds(p, 8)] = done.reshape(8, STRIP, nz)
+
+    def finish(u):
+        slot = u % 2
+        s, h = divmod(u, strips)
+        part = pl.ds(h * STRIP, STRIP)
+        for d in range(2):
+            z_copy(u, d).wait_recv()
         halves = []
         for f in range(2):
-            packed = jnp.concatenate(
-                [zrecv[s, 0, pl.ds(f * ny, ny)], zrecv[s, 1, pl.ds(f * ny, ny)]], axis=1)
+            own = pl.ds(f * STRIP, STRIP)
+            packed = jnp.concatenate([zrecv[u, 0, own], zrecv[u, 1, own]], axis=1)
             halves.append(jnp.concatenate(split(packed), axis=0))
         for p in range(0, nx, 2):
-            level = [None, None]
+            level = []
             for f, (radius, less) in enumerate(zip(RADII, (0.3, 0.1))):
                 done = jnp.dot(halves[f], wh[f, p // 2], preferred_element_type=F32)
-                done = done[:ny] + done[ny:]
+                done = done[:STRIP] + done[STRIP:]
                 pair = []
                 for j in range(2):
                     smooth = (zm[slot, f, p + j] + done[:, j * nz:(j + 1) * nz]) * scale_of(radius)
-                    pair.append(effv[p + j] * smooth - less)
-                level[f] = pair
+                    pair.append(effv[p + j, part] * smooth - less)
+                level.append(pair)
             for j in range(2):
-                outv[s, p + j] = jnp.maximum(level[0][j], level[1][j])
-        out_copy(s).start()
-
+                top = jnp.maximum(level[0][j], level[1][j])
+                outv[s, p + j, part] = jnp.clip(0.5 + 0.25 * top, 0.0, 1.0)
+        if out is not None:
+            out_copy(u).start()
+
+    units = snaps * strips
     for s in range(snaps):
         own_copy(s).wait()
         for d in range(2):
@@ -234,61 +249,68 @@
                 f_copy(s, q, d).wait_recv()
         for g in edge:
             smooth_x(s, g)
-        for g in inner:
-            for d in range(2):
-                x_copy(s, g, d).wait_recv()
-            smooth_x(s, g)
-        smooth_y(s)
-        main_z(s)
-        if s == 0:
-            eff_copy.wait()
-        else:
-            finish(s - 1)
-    finish(snaps - 1)
+        ready = 1
+        for h in range(strips):
+            last = min(((h + 1) * STRIP + 2 * H) // GROUP, groups - 1)
+            for g in range(ready, last):
+                for d in range(2):
+                    x_copy(s, g, d).wait_recv()
+                smooth_x(s, g)
+            ready = max(ready, last)
+            u = s * strips + h
+            smooth_y(u)
+            main_z(u)
+            if u == 0:
+                eff_copy.wait()
+            else:
+                finish(u - 1)
+    finish(units - 1)
 
     for s in range(snaps):
         for d in range(2):
             for g in range(groups):
                 x_copy(s, g, d).wait_send()
             y_copy(s, d).wait_send()
-            z_copy(s, d).wait_send()
             for q in range(2):
                 f_copy(s, q, d).wait_send()
-        out_copy(s).wait()
+    for u in range(units):
+        for d in range(2):
+            z_copy(u, d).wait_send()
+        if out is not None:
+            out_copy(u).wait()
 
 
 def on_device(density, efficiency):
     snaps, nx, ny, nz = density.shape
     rows = ny + 2 * H
     groups = rows // GROUP
+    units = snaps * (ny // STRIP)
     dma = pltpu.SemaphoreType.DMA
-    level = pl.pallas_call(
+    return pl.pallas_call(
         kernel,
-        out_shape=jax.ShapeDtypeStruct(density.shape, F32),
+        out_shape=pltpu.VMEM(density.shape, F32),
         in_specs=[pl.BlockSpec(memory_space=pl.ANY)] * 2,
-        out_specs=pl.BlockSpec(memory_space=pl.ANY),
+        out_specs=pl.BlockSpec(memory_space=pltpu.VMEM),
         scratch_shapes=[
             pltpu.VMEM((snaps, nx + 2 * H, rows, nz), F32),
             pltpu.VMEM((nx, ny, nz), F32),
             pltpu.VMEM((2, nx, 2 * rows, nz), BF16),
-            pltpu.VMEM((2, nx, ny, 2 * nz), BF16),
-            pltpu.VMEM((2, 2, nx, ny, nz), F32),
-            pltpu.VMEM((snaps, 2, 2 * ny, nx * H), F32),
-            pltpu.VMEM((snaps, 2, 2 * ny, nx * H), F32),
-            pltpu.VMEM((2, ny, 2 * rows), BF16),
+            pltpu.VMEM((2, nx, STRIP, 2 * nz), BF16),
+            pltpu.VMEM((2, 2, nx, STRIP, nz), F32),
+            pltpu.VMEM((units, 2, 2 * STRIP, nx * H), F32),
+            pltpu.VMEM((units, 2, 2 * STRIP, nx * H), F32),
+            pltpu.VMEM((2, STRIP, 2 * (STRIP + 2 * H)), BF16),
             pltpu.VMEM((2, 2 * nz, nz), BF16),
             pltpu.VMEM((2, nx // 2, 2 * nx * H, 2 * nz), BF16),
-            pltpu.VMEM((snaps, nx, ny, nz), F32),
             dma((snaps, groups, 2)), dma((snaps, groups, 2)),
             dma((snaps, 2)), dma((snaps, 2)),
             dma((snaps, 2, 2)), dma((snaps, 2, 2)),
-            dma((snaps, 2)), dma((snaps, 2)),
-            dma((snaps,)), dma, dma((snaps,)),
+            dma((units, 2)), dma((units, 2)),
+            dma((snaps,)), dma, dma((units,)),
         ],
         compiler_params=pltpu.CompilerParams(
             collective_id=0, has_side_effects=True),
     )(density, efficiency)
-    return jnp.clip(0.5 + 0.25 * level, 0.0, 1.0)
 
 
 def solution(mesh):

time: 51.7 us -> 47.9 us (0.926)
  other arithmetic: 2.86 us -> 0 us
  Pallas kernels: 48.7 us -> 46.6 us
  local copies, waits for them, and re-layouts: 0 us -> 1.15 us
    min x1 -> x0, other arithmetic: 2.86 us -> none  [on_device(): return jnp.clip(0.5 + 0.25 * level, 0.0, 1.0)]
    pallas_call x1, Pallas kernels: 48.7 us -> 46.6 us  [on_device(): pl.pallas_call(kernel, out_shape=pltpu.VMEM(density.shape, F32), in_specs...]
    unnamed x0 -> x1, local copies, waits for them, and re-layouts: none -> 1.15 us
where the time goes in v2:
time: 47.9 us; the launch traced here: 47.7 us
  Pallas kernels  46.6 us (97%)
  local copies, waits for them, and re-layouts  1.15 us (2%)
    pallas_call x1, Pallas kernels, on_device(): pl.pallas_call(kernel, out_shape=pltpu.VMEM(density.shape, F32), in_specs...  46.6 us
    unnamed x1, local copies, waits for them, and re-layouts  1.15 us

profile of v2, /device:TPU:0, one launch (start us, length us, event | category | flops | bytes accessed | tf_op | source)
XLA Modules:
  0.0 47.7 jit_solution(3889461620942450941)
XLA Ops:
  0.0 46.6 %shard_map.28 = f32[3,16,64,128]{3,2,1,0:T(8,128)S(1)} custom-call(f32[3,16,64,128]{3,2,1,0:T(8,128)} %dens.1, f32[16,64,128]{2,1,0:T(8,128)} %eff.1), custom_call_target="tpu_custom_call" | custom-call | tf_op jit(solution)/shard_map/pallas_call | solution.py:289
  46.6 1.1 %copy.4 = f32[3,16,64,128]{3,2,1,0:T(8,128)} copy(f32[3,16,64,128]{3,2,1,0:T(8,128)S(1)} %shard_map.28) | data formatting | bytes 3145728

commit v3 on v2

--- a/solution.py
+++ b/solution.py
@@ -38,10 +38,9 @@
     return lax.broadcasted_iota(jnp.int32, shape, dim)
 
 
-def kernel(dens, eff, outv, ext, effv, xb, zb, zm, zsend, zrecv, wy, wm, wh,
-           x_send, x_recv, y_send, y_recv, f_send, f_recv, z_send, z_recv,
-           own_sem, eff_sem, out_sem):
-    out = None
+def kernel(dens, eff, outv, ext, effv, xb, zb, zm, zsend, zrecv, wy, wm, wh, near_x, tsend, trecv,
+           x_send, x_recv, y_send, y_recv, f_send, f_recv, z_send, z_recv, t_send, t_recv,
+           own_sem, eff_sem):
     snaps, nx, ny, nz = dens.shape
     rows = ny + 2 * H
     groups = rows // GROUP
@@ -59,28 +58,34 @@
 
     eff_copy = pltpu.make_async_copy(eff, effv, eff_sem)
 
-    def out_copy(u):
-        s, h = divmod(u, strips)
-        part = pl.ds(h * STRIP, STRIP)
-        return pltpu.make_async_copy(outv.at[s, :, part], out.at[s, :, part], out_sem.at[u])
-
-    def group_rows(g):
-        if g == 0:
-            return 0, H
-        if g == groups - 1:
-            return ny - H, H
-        return g * GROUP - H, GROUP
-
-    def x_copy(s, g, d):
-        start, size = group_rows(g)
+    final = snaps - 1
+    edge = (0, groups - 1)
+    inner = tuple(range(1, groups - 1))
+    last = inner[-1]
+    first_needed = (strips - 1) * STRIP // GROUP
+    ordered = tuple(sorted(inner, key=lambda g: (g == last, g < first_needed)))
+
+    def arrivals(s):
+        return tuple((g,) for g in ordered) if s == final else (inner,)
+
+    def x_copy(s, together, d):
+        start = max(together[0] * GROUP - H, 0)
+        size = min((together[-1] + 1) * GROUP - H, ny) - start
         source = nx - H if d == 0 else 0
         target = 0 if d == 0 else nx + H
+        g = together[0]
         return pltpu.make_async_remote_copy(
             src_ref=dens.at[s, pl.ds(source, H), pl.ds(start, size)],
             dst_ref=ext.at[s, pl.ds(target, H), pl.ds(H + start, size)],
             send_sem=x_send.at[s, g, d], recv_sem=x_recv.at[s, g, d],
             device_id={"gx": near["gx"][d]}, device_id_type=MESH)
 
+    def t_copy(d):
+        return pltpu.make_async_remote_copy(
+            src_ref=tsend.at[d], dst_ref=trecv.at[d],
+            send_sem=t_send.at[d], recv_sem=t_recv.at[d],
+            device_id={"gx": near["gx"][d]}, device_id_type=MESH)
+
     def y_copy(s, d):
         source = ny - H if d == 0 else 0
         target = 0 if d == 0 else ny + H
@@ -117,19 +122,29 @@
                 barrier, inc=1, device_id={axis: near[axis][d]}, device_id_type=MESH)
     pl.semaphore_wait(barrier, 6)
 
-    edge = (0, groups - 1)
-    inner = tuple(range(1, groups - 1))
     for s in range(snaps):
         for g in edge:
             for d in range(2):
-                x_copy(s, g, d).start()
+                x_copy(s, (g,), d).start()
     for s in range(snaps):
         for d in range(2):
             y_copy(s, d).start()
-    for s in range(snaps):
-        for g in inner:
+
+    own_copy(final).wait()
+    last_rows = pl.ds(last * GROUP, GROUP)
+    pieces = lax.div(iota((GROUP, nz), 1), 2 * H)
+    for d in range(2):
+        packed = jnp.zeros((GROUP, nz), F32)
+        for p in range(H):
+            plane = ext[final, (nx if d == 0 else H) + p, last_rows]
+            packed = jnp.where(pieces == p, pltpu.roll(plane, p * 2 * H + H, 1), packed)
+        tsend[d] = packed
+        t_copy(d).start()
+
+    for s in range(snaps):
+        for together in arrivals(s):
             for d in range(2):
-                x_copy(s, g, d).start()
+                x_copy(s, together, d).start()
 
     for f, radius in enumerate(RADII):
         shape = (STRIP, wide)
@@ -154,15 +169,15 @@
     for s in range(snaps):
         for d, g in ((0, groups - 1), (1, 0)):
             for q in range(2):
-                x_copy(s, g, q).wait_recv()
+                x_copy(s, (g,), q).wait_recv()
                 f_copy(s, q, d).start()
 
-    def smooth_x(s, g):
+    def smooth_x(field, start, g):
         base = g * GROUP
 
         def one(i, carry):
             def plane(k):
-                return ext[s, i + (H + k), pl.ds(base, GROUP)]
+                return field[i + (H + k), pl.ds(start, GROUP)]
 
             center = plane(0)
             sums = [center * float((radius + 1) ** 2) for radius in RADII]
@@ -181,7 +196,7 @@
 
     slots = lax.div(iota((STRIP, nz), 1), H)
 
-    def smooth_y(u):
+    def smooth_y(u, keep=True, send=True):
         base = (u % strips) * STRIP
         for f in range(2):
             up = jnp.zeros((STRIP, nz), F32)
@@ -194,16 +209,20 @@
                 done = jnp.dot(wy[f], both, preferred_element_type=F32)
                 for j in range(2):
                     value = done[:, j * nz:(j + 1) * nz]
-                    rolled = pltpu.roll(value, ((p + j + 1) * H) % nz, 1)
-                    up = jnp.where(slots == p + j, rolled, up)
-                    down = jnp.where(slots == (p + j + 1) % nx, rolled, down)
-                    high, low = split(value)
-                    zb[f, p + j, :, pl.ds(0, nz)] = high
-                    zb[f, p + j, :, pl.ds(nz, nz)] = low
-            zsend[u, 0, pl.ds(f * STRIP, STRIP)] = up
-            zsend[u, 1, pl.ds(f * STRIP, STRIP)] = down
-        for d in range(2):
-            z_copy(u, d).start()
+                    if send:
+                        rolled = pltpu.roll(value, ((p + j + 1) * H) % nz, 1)
+                        up = jnp.where(slots == p + j, rolled, up)
+                        down = jnp.where(slots == (p + j + 1) % nx, rolled, down)
+                    if keep:
+                        high, low = split(value)
+                        zb[f, p + j, :, pl.ds(0, nz)] = high
+                        zb[f, p + j, :, pl.ds(nz, nz)] = low
+            if send:
+                zsend[u, 0, pl.ds(f * STRIP, STRIP)] = up
+                zsend[u, 1, pl.ds(f * STRIP, STRIP)] = down
+        if send:
+            for d in range(2):
+                z_copy(u, d).start()
 
     def main_z(u):
         slot = u % 2
@@ -237,47 +256,64 @@
             for j in range(2):
                 top = jnp.maximum(level[0][j], level[1][j])
                 outv[s, p + j, part] = jnp.clip(0.5 + 0.25 * top, 0.0, 1.0)
-        if out is not None:
-            out_copy(u).start()
 
     units = snaps * strips
-    for s in range(snaps):
-        own_copy(s).wait()
+
+    def outer_lanes_ahead():
+        for d in range(2):
+            t_copy(d).wait_recv()
+            packed = trecv[d]
+            for p in range(H):
+                near_x[(0 if d == 0 else nx + H) + p] = pltpu.roll(
+                    packed, nz - p * 2 * H - H, 1)
+        for p in range(nx):
+            near_x[H + p] = ext[final, H + p, last_rows]
+        smooth_x(near_x, 0, last)
+        smooth_y(units - 1, keep=False)
+
+    for s in range(snaps):
+        if s != final:
+            own_copy(s).wait()
         for d in range(2):
             y_copy(s, d).wait_recv()
             for q in range(2):
                 f_copy(s, q, d).wait_recv()
         for g in edge:
-            smooth_x(s, g)
-        ready = 1
-        for h in range(strips):
-            last = min(((h + 1) * STRIP + 2 * H) // GROUP, groups - 1)
-            for g in range(ready, last):
-                for d in range(2):
-                    x_copy(s, g, d).wait_recv()
-                smooth_x(s, g)
-            ready = max(ready, last)
-            u = s * strips + h
-            smooth_y(u)
-            main_z(u)
-            if u == 0:
-                eff_copy.wait()
-            else:
-                finish(u - 1)
+            smooth_x(ext.at[s], g * GROUP, g)
+        held = set(edge)
+        done = 0
+        for together in arrivals(s):
+            for d in range(2):
+                x_copy(s, together, d).wait_recv()
+            for g in together:
+                smooth_x(ext.at[s], g * GROUP, g)
+            held.update(together)
+            if s == final and held == set(range(first_needed, groups)) - {last} | set(edge):
+                outer_lanes_ahead()
+            while done < strips and held.issuperset(
+                    range(done * STRIP // GROUP, (done * STRIP + wide) // GROUP)):
+                u = s * strips + done
+                smooth_y(u, send=u != units - 1)
+                main_z(u)
+                if u == 0:
+                    eff_copy.wait()
+                else:
+                    finish(u - 1)
+                done += 1
     finish(units - 1)
 
     for s in range(snaps):
         for d in range(2):
-            for g in range(groups):
-                x_copy(s, g, d).wait_send()
+            for together in tuple((g,) for g in edge) + arrivals(s):
+                x_copy(s, together, d).wait_send()
             y_copy(s, d).wait_send()
             for q in range(2):
                 f_copy(s, q, d).wait_send()
+    for d in range(2):
+        t_copy(d).wait_send()
     for u in range(units):
         for d in range(2):
             z_copy(u, d).wait_send()
-        if out is not None:
-            out_copy(u).wait()
 
 
 def on_device(density, efficiency):
@@ -302,11 +338,15 @@
             pltpu.VMEM((2, STRIP, 2 * (STRIP + 2 * H)), BF16),
             pltpu.VMEM((2, 2 * nz, nz), BF16),
             pltpu.VMEM((2, nx // 2, 2 * nx * H, 2 * nz), BF16),
+            pltpu.VMEM((nx + 2 * H, GROUP, nz), F32),
+            pltpu.VMEM((2, GROUP, nz), F32),
+            pltpu.VMEM((2, GROUP, nz), F32),
             dma((snaps, groups, 2)), dma((snaps, groups, 2)),
             dma((snaps, 2)), dma((snaps, 2)),
             dma((snaps, 2, 2)), dma((snaps, 2, 2)),
             dma((units, 2)), dma((units, 2)),
-            dma((snaps,)), dma, dma((units,)),
+            dma((2,)), dma((2,)),
+            dma((snaps,)), dma,
         ],
         compiler_params=pltpu.CompilerParams(
             collective_id=0, has_side_effects=True),

time: 47.9 us -> 46.2 us (0.965)
  Pallas kernels: 46.6 us -> 44.9 us
    pallas_call x1, Pallas kernels: 46.6 us -> 44.9 us  [on_device(): pl.pallas_call(kernel, out_shape=pltpu.VMEM(density.shape, F32), in_specs...]
where the time goes in v3:
time: 46.2 us; the launch traced here: 46 us
  Pallas kernels  44.9 us (97%)
  local copies, waits for them, and re-layouts  1.15 us (2%)
    pallas_call x1, Pallas kernels, on_device(): pl.pallas_call(kernel, out_shape=pltpu.VMEM(density.shape, F32), in_specs...  44.9 us
    unnamed x1, local copies, waits for them, and re-layouts  1.15 us

profile of v3, /device:TPU:0, one launch (start us, length us, event | category | flops | bytes accessed | tf_op | source)
XLA Modules:
  0.0 46.0 jit_solution(11521168772142794855)
XLA Ops:
  0.0 44.9 %shard_map.28 = f32[3,16,64,128]{3,2,1,0:T(8,128)S(1)} custom-call(f32[3,16,64,128]{3,2,1,0:T(8,128)} %dens.1, f32[16,64,128]{2,1,0:T(8,128)} %eff.1), custom_call_target="tpu_custom_call" | custom-call | tf_op jit(solution)/shard_map/pallas_call | solution.py:325
  44.9 1.1 %copy.4 = f32[3,16,64,128]{3,2,1,0:T(8,128)} copy(f32[3,16,64,128]{3,2,1,0:T(8,128)S(1)} %shard_map.28) | data formatting | bytes 3145728

commit v4 on v3

--- a/solution.py
+++ b/solution.py
@@ -122,10 +122,23 @@
                 barrier, inc=1, device_id={axis: near[axis][d]}, device_id_type=MESH)
     pl.semaphore_wait(barrier, 6)
 
-    for s in range(snaps):
-        for g in edge:
-            for d in range(2):
-                x_copy(s, (g,), d).start()
+    at_top = lax.axis_index("gx") == lax.axis_size("gx") - 1
+
+    def start_pieces(pieces, first):
+        for piece in pieces:
+            x_copy(*piece, first).start()
+            x_copy(*piece, 1 - first).start()
+
+    def send_x(pieces):
+        @pl.when(at_top)
+        def _():
+            start_pieces(pieces, 0)
+
+        @pl.when(jnp.logical_not(at_top))
+        def _():
+            start_pieces(pieces, 1)
+
+    send_x([(s, (g,)) for s in range(snaps) for g in edge])
     for s in range(snaps):
         for d in range(2):
             y_copy(s, d).start()
@@ -141,10 +154,7 @@
         tsend[d] = packed
         t_copy(d).start()
 
-    for s in range(snaps):
-        for together in arrivals(s):
-            for d in range(2):
-                x_copy(s, together, d).start()
+    send_x([(s, together) for s in range(snaps) for together in arrivals(s)])
 
     for f, radius in enumerate(RADII):
         shape = (STRIP, wide)
@@ -192,7 +202,7 @@
                 xb[f, i, pl.ds(rows + base, GROUP)] = low
             return carry
 
-        lax.fori_loop(0, nx, one, 0, unroll=4)
+        lax.fori_loop(0, nx, one, 0, unroll=16)
 
     slots = lax.div(iota((STRIP, nz), 1), H)
 

time: 46.2 us -> 45.9 us (level)
  no operation moved by 1% of the time
where the time goes in v4:
time: 45.9 us; the launch traced here: 45.8 us
  Pallas kernels  44.6 us (97%)
  local copies, waits for them, and re-layouts  1.15 us (3%)
    pallas_call x1, Pallas kernels, on_device(): pl.pallas_call(kernel, out_shape=pltpu.VMEM(density.shape, F32), in_specs...  44.6 us
    unnamed x1, local copies, waits for them, and re-layouts  1.15 us

profile of v4, /device:TPU:0, one launch (start us, length us, event | category | flops | bytes accessed | tf_op | source)
XLA Modules:
  0.0 45.8 jit_solution(5093537823011868977)
XLA Ops:
  0.0 44.6 %shard_map.28 = f32[3,16,64,128]{3,2,1,0:T(8,128)S(1)} custom-call(f32[3,16,64,128]{3,2,1,0:T(8,128)} %dens.1, f32[16,64,128]{2,1,0:T(8,128)} %eff.1), custom_call_target="tpu_custom_call" | custom-call | tf_op jit(solution)/shard_map/pallas_call | solution.py:335
  44.6 1.1 %copy.4 = f32[3,16,64,128]{3,2,1,0:T(8,128)} copy(f32[3,16,64,128]{3,2,1,0:T(8,128)S(1)} %shard_map.28) | data formatting | bytes 3145728
